TPU v7x, 256 devices: a whole 4x4x8 slice. The times are simulated.
256 devices in a mesh: rep: 4 (over z_lo, core), shard: 64 (over z_hi, y, x).
Axes of the slice: x: 4, y: 4, z: 8 (z_hi: 4, z_lo: 2; z = z_hi * 2 + z_lo), core: 2. Of those that a mesh axis runs over, the one named last changes fastest.
Arguments:
- conv_input: bfloat16 [256, 256, 6144], P(('rep', 'shard')), may hold values from -24 to 24
- cotangent: bfloat16 [256, 256, 6144], P(('rep', 'shard')), may hold values from -24 to 24
- kernel: bfloat16 [31, 6144], P(None, 'shard'), may hold values from -1 to 1
- conv_bias: bfloat16 [6144], P('shard'), may hold values from -3 to 3
- ln_gain: bfloat16 [6144], P('shard'), may hold values from 0.25 to 1.75
- ln_bias: bfloat16 [6144], P('shard'), may hold values from -3 to 3
Outputs:
- activated: bfloat16 [256, 256, 6144], P(('rep', 'shard'))
- grad_input: bfloat16 [256, 256, 6144], P(('rep', 'shard'))
- grad_kernel: float32 [31, 6144], P(None, 'shard')
- grad_conv_bias: float32 [6144], P('shard')
- grad_gain: float32 [6144], P('shard')
- grad_ln_bias: float32 [6144], P('shard')
All inputs are finite; a program needn't handle non-finite values.
Results may differ from a plain program's by a relative error of at most 0.0012.
Values may be sent and summed in bfloat16 or wider, within the bound.
No kernel may reach another device: no remote copies, remote signals or barrier semaphores. Data moves between devices by JAX's collectives and lax.ppermute only.
A program may use at most 128 MiB of HBM per device.

v0:
```python
import math
import jax
import jax.numpy as jnp
from jax import lax
from jax.sharding import PartitionSpec as P


def forward_part(frames_in, params):
    taps = params.shape[0] - 3
    half_width = (taps - 1) // 2
    length = frames_in.shape[0]
    padded = jnp.pad(frames_in, ((half_width, half_width), (0, 0)))
    conv_out = params[taps].astype(jnp.float32)[None, :] + params[0].astype(jnp.float32) * padded[
        0:length
    ].astype(jnp.float32)
    for lag_index in range(1, taps):
        conv_out = conv_out + params[lag_index].astype(jnp.float32) * padded[
            lag_index : lag_index + length
        ].astype(jnp.float32)
    row_mean = jnp.mean(conv_out, axis=-1, keepdims=True)
    centered = conv_out - row_mean
    inverse = lax.rsqrt(jnp.mean(centered * centered, axis=-1, keepdims=True) + 1e-05)
    normed = centered * inverse
    affine = params[taps + 1].astype(jnp.float32) * normed + params[taps + 2].astype(jnp.float32)
    squash = jax.nn.sigmoid(affine)
    activated = (affine * squash).astype(jnp.bfloat16)
    return (activated, normed, inverse, affine, squash)


def backward_part(frames_in, upstream, params, normed, inverse, affine, squash):
    taps = params.shape[0] - 3
    half_width = (taps - 1) // 2
    length = frames_in.shape[0]
    grad_affine = upstream.astype(jnp.float32) * squash * (1.0 + affine * (1.0 - squash))
    grad_normed = grad_affine * params[taps + 1].astype(jnp.float32)
    grad_conv = inverse * (
        grad_normed
        - jnp.mean(grad_normed, axis=-1, keepdims=True)
        - normed * jnp.mean(grad_normed * normed, axis=-1, keepdims=True)
    )
    padded_in = jnp.pad(frames_in, ((half_width, half_width), (0, 0)))
    kernel_rows = [
        jnp.sum(grad_conv * padded_in[lag_index : lag_index + length].astype(jnp.float32), axis=0)
        for lag_index in range(taps)
    ]
    padded_grad = jnp.pad(grad_conv, ((half_width, half_width), (0, 0)))
    back_start = 2 * half_width
    grad_input = params[0].astype(jnp.float32) * padded_grad[back_start : back_start + length]
    for lag_index in range(1, taps):
        first = back_start - lag_index
        grad_input = (
            grad_input + params[lag_index].astype(jnp.float32) * padded_grad[first : first + length]
        )
    terms = jnp.concatenate(
        [
            jnp.stack(kernel_rows, 0),
            jnp.sum(grad_conv, axis=0)[None],
            jnp.sum(grad_affine * normed, axis=0)[None],
            jnp.sum(grad_affine, axis=0)[None],
        ],
        0,
    )
    return (grad_input.astype(jnp.bfloat16), terms)


def per_device(conv_input, cotangent, kernel, conv_bias, ln_gain, ln_bias):
    taps = kernel.shape[0]
    packed = jnp.concatenate([kernel, conv_bias[None], ln_gain[None], ln_bias[None]], 0)
    gathered = lax.all_gather(packed, "shard", axis=1, tiled=True)
    activated, normed, inverse, affine, squash = jax.vmap(forward_part, in_axes=(0, None))(
        conv_input, gathered
    )
    again = lax.all_gather(packed, "shard", axis=1, tiled=True)
    grad_input, terms = jax.vmap(backward_part, in_axes=(0, 0, None, 0, 0, 0, 0))(
        conv_input, cotangent, again, normed, inverse, affine, squash
    )
    terms = jnp.sum(terms, axis=0)
    replicas = lax.axis_size("rep")
    groups = lax.axis_size("shard")
    share_sum = lax.psum_scatter(terms, "shard", scatter_dimension=1, tiled=True)
    summed = lax.psum(share_sum, "rep")
    factor = 1.0 / math.sqrt(conv_input.shape[0] * conv_input.shape[1] * replicas * groups)
    grads = summed * factor
    return (activated, grad_input, grads[:taps], grads[taps], grads[taps + 1], grads[taps + 2])


def solution(mesh):
    in_specs = (
        P(("rep", "shard"), None, None),
        P(("rep", "shard"), None, None),
        P(None, "shard"),
        P("shard"),
        P("shard"),
        P("shard"),
    )
    out_specs = (
        P(("rep", "shard"), None, None),
        P(("rep", "shard"), None, None),
        P(None, "shard"),
        P("shard"),
        P("shard"),
        P("shard"),
    )
    return jax.shard_map(
        per_device, mesh=mesh, in_specs=in_specs, out_specs=out_specs, check_vma=False
    )
```

profile of v0, /device:TPU:1, one launch (start us, length us, event | category | flops | bytes accessed | tf_op | source)
XLA Modules:
  0.0 571.3 jit_solution(10006896554556620029)
XLA Ops:
  7.2 0.0 copy-start.2
  7.2 0.0 reduce-scatter.4.cloned.1.call-start
  7.2 0.9 maximum_bitcast_fusion.1
  8.1 171.1 %all-gather = bf16[64,96,34]{1,2,0:T(8,128)(2,1)S(1)} all-gather(bf16[1,96,34]{1,2,0:T(8,128)(2,1)S(1)} %maximum_bitcast_fusion.1), channel_id=1, replica_groups=mesh['rep'=4,'shard'=64] {'shard'}, dimensions={0}, use_global_device_ids=true | all-gather | bytes 424320 | tf_op jit(solution)/shard_map/all_gather | solution.py:69
  179.2 0.9 copy.13
  180.1 2.6 reshape.462
  182.8 2.5 slice_convert_fusion.32
  185.3 3.1 slice_convert_fusion.33
  188.4 0.0 copy-done.2
  188.4 37.1 %fusion.123 = (f32[256]{0:T(256)S(1)}, f32[1,256,6144]{2,1,0:T(8,128)}) fusion(f32[6144]{0:T(1024)S(1)} %bitcast.121, f32[6144]{0:T(1024)S(1)} %bitcast.123, f32[6144]{0:T(1024)} %bitcast.125, f32[6144]{0:T(1024)} %bitcast.127, f32[6144]{0:T(1024)} %bitcast.129, f32[6144]{0:T(1024)} %bitcast.131, f32[6144]{0:T(1024)} %bitcast.133, f32[6144]{0:T(1024)} %bitcast.135, ...), kind=kLoop, calls=%fused_computation.269 | loop fusion | flops 147848960 | bytes 10224640 | tf_op jit(solution)/shard_map/vmap()/reduce_sum | solution.py:20
  225.5 0.0 copy-start.1
  225.5 3.7 multiply_reduce_fusion.2
  229.3 0.9 copy-done.1
  230.1 0.0 copy-start.18
  230.1 9.2 %multiply_reduce_fusion = (f32[6144]{0:T(1024)}, f32[256]{0:T(256)S(1)}, f32[256]{0:T(256)S(1)}, f32[6144]{0:T(1024)}, f32[1,256,6144]{2,1,0:T(8,128)S(1)}, /*index=5*/bf16[1,256,6144]{2,1,0:T(8,128)(2,1)}) fusion(f32[1,256,6144]{2,1,0:T(8,128)S(1)} %copy-done.1, f32[256]{0:T(256)S(1)} %add_rsqrt_fusion, f32[256]{0:T(256)S(1)} %broadcast_multiply_fusion.3, ...), kind=kLoop, calls=%fused_computation.215 | loop fusion | flops 34590208 | bytes 18976768 | tf_op jit(solution)/shard_map/vmap()/reduce_sum | solution.py:58
  239.4 0.0 copy-done.18
  239.4 11.6 %fusion.122 = (f32[6144]{0:T(1024)}, f32[6144]{0:T(1024)}, f32[6144]{0:T(1024)}, f32[6144]{0:T(1024)}, f32[6144]{0:T(1024)}, /*index=5*/f32[6144]{0:T(1024)}, f3...) fusion(bf16[1,256,6144]{2,1,0:T(8,128)(2,1)S(1)} %copy-done.2, f32[256]{0:T(256)S(1)} %get-tuple-element.84, ...), kind=kLoop, calls=%fused_computation.214 | loop fusion | flops 53422080 | bytes 22269952 | tf_op jit(solution)/shard_map/vmap()/reduce_sum | solution.py:43
  251.0 0.0 copy-start
  251.0 4.3 fusion.89
  255.3 8.5 %fusion.98 = (f32[6144]{0:T(1024)}, f32[6144]{0:T(1024)}, f32[6144]{0:T(1024)}, f32[6144]{0:T(1024)}, f32[6144]{0:T(1024)}, /*index=5*/f32[6144]{0:T(1024)}, f32[6144]{0:T(1024)}, f32[6144]{0:T(1024)}, f32[6144]{0:T(1024)}) fusion(f32[1,256,6144]{2,1,0:T(8,128)S(1)} %get-tuple-element.42, bf16[1,256,6144]{2,1,0:T(8,128)(2,1)S(1)} %copy-done.2), kind=kLoop, calls=%fused_computation.190 | loop fusion | flops 42412032 | bytes 9658368 | tf_op jit(solution)/shard_map/vmap()/reduce_sum | solution.py:43
  263.8 0.0 copy-done
  263.8 8.9 %fusion.107 = (f32[6144]{0:T(1024)}, f32[6144]{0:T(1024)}, f32[6144]{0:T(1024)}, f32[6144]{0:T(1024)}, f32[6144]{0:T(1024)}, /*index=5*/f32[6144]{0:T(1024)}, f3...) fusion(f32[1,256,6144]{2,1,0:T(8,128)S(1)} %get-tuple-element.42, bf16[1,256,6144]{2,1,0:T(8,128)(2,1)S(1)} %copy-done.2), kind=kLoop, calls=%fused_computation.199 | loop fusion | flops 43978752 | bytes 9682944 | tf_op jit(solution)/shard_map/vmap()/reduce_sum | solution.py:43
  272.7 0.0 copy-start.3
  272.7 0.0 copy-start.4
  272.7 0.0 copy-start.5
  272.7 0.0 copy-start.6
  272.7 0.0 copy-start.7
  272.8 0.0 copy-start.8
  272.8 0.0 copy-start.9
  272.8 0.0 copy-start.10
  272.8 0.0 copy-start.11
  272.8 0.0 copy-start.12
  272.8 0.0 copy-start.13
  272.8 0.0 copy-start.14
  272.8 0.0 copy-start.15
  272.8 0.0 copy-start.16
  272.8 0.0 copy-start.17
  272.9 4.5 stack.127
  277.4 0.9 maximum_bitcast_fusion
  278.3 2.3 copy.14
  280.6 0.0 reduce-scatter.4.cloned.1.call-update
  280.6 0.0 copy-done.3
  280.7 0.0 copy-done.4
  280.7 0.0 copy-done.5
  280.7 0.0 copy-done.6
  280.7 0.0 copy-done.7
  280.7 0.0 copy-done.8
  280.7 0.0 copy-done.9
  280.7 0.0 copy-done.10
  280.7 0.0 copy-done.11
  280.7 0.0 copy-done.12
  280.7 0.0 copy-done.13
  280.8 0.0 copy-done.14
  280.8 0.0 copy-done.15
  280.8 0.0 copy-done.16
  280.8 0.0 copy-done.17
  280.8 88.0 %fusion.54 = bf16[1,256,6144]{2,1,0:T(8,128)(2,1)} fusion(f32[1,256,6144]{2,1,0:T(8,128)} %copy-done, f32[6144]{0:T(1024)S(1)} %bitcast.122, f32[6144]{0:T(1024)S(1)} %bitcast.124, f32[6144]{0:T(1024)S(1)} %bitcast.126, f32[6144]{0:T(1024)S(1)} %bitcast.128, f32[6144]{0:T(1024)S(1)} %bitcast.130, f32[6144]{0:T(1024)S(1)} %bitcast.132, ...), kind=kLoop, calls=%fused_computation.146 | loop fusion | flops 97517568 | bytes 10199040 | tf_op jit(solution)/shard_map/vmap()/convert_element_type | solution.py:63
  368.8 181.7 %reduce-scatter.4.cloned.1.call-done = f32[96,34]{1,0:T(8,128)} async-done(((f32[6144,34]{1,0:T(8,128)}), f32[96,34]{1,0:T(8,128)}) %reduce-scatter.4.cloned.1.call-update) | async-done | bytes 13072
  550.6 0.9 copy.15
  551.4 11.9 %psum.7 = f32[34,96]{1,0:T(8,128)S(1)} all-reduce(f32[34,96]{1,0:T(8,128)S(1)} %copy.15), channel_id=1, replica_groups=mesh['rep'=4,'shard'=64] {'rep'}, use_global_device_ids=true, to_apply=%region_39.40 | all-reduce | flops 3264 | bytes 26112 | tf_op jit(solution)/shard_map/psum | solution.py:81
  563.3 0.5 slice_bitcast_fusion
  563.9 0.6 slice.491
  (4 shorter events, 0.0 us)
Async XLA Ops:
  7.2 181.2 %copy-start.2 = (bf16[1,256,6144]{2,1,0:T(8,128)(2,1)S(1)}, bf16[1,256,6144]{2,1,0:T(8,128)(2,1)}, u32[]{:S(2)}) copy-start(bf16[1,256,6144]{2,1,0:T(8,128)(2,1)} %param.6) | copy-start | bytes 9437188
  7.2 543.4 %reduce-scatter.4.cloned.1.call-start = ((), (), s32[]{:S(2)}) async-start(), calls=%async_computation.1 | async-start | bytes 3194880
  225.5 4.6 copy-start.1
  230.1 9.2 %copy-start.18 = (f32[1,6144]{1,0:T(1,128)S(1)}, f32[1,6144]{1,0:T(1,128)}, u32[]{:S(2)}) copy-start(f32[1,6144]{1,0:T(1,128)} %get-tuple-element.47) | copy-start | bytes 73732
  251.0 12.8 %copy-start = (f32[1,256,6144]{2,1,0:T(8,128)}, f32[1,256,6144]{2,1,0:T(8,128)S(1)}, u32[]{:S(2)}) copy-start(f32[1,256,6144]{2,1,0:T(8,128)S(1)} %get-tuple-element.42) | copy-start | bytes 18874372
  272.7 7.9 %copy-start.3 = (f32[1,6144]{1,0:T(1,128)S(1)}, f32[1,6144]{1,0:T(1,128)}, u32[]{:S(2)}) copy-start(f32[1,6144]{1,0:T(1,128)} %get-tuple-element.51) | copy-start | bytes 73732
  272.7 7.9 %copy-start.4 = (f32[1,6144]{1,0:T(1,128)S(1)}, f32[1,6144]{1,0:T(1,128)}, u32[]{:S(2)}) copy-start(f32[1,6144]{1,0:T(1,128)} %get-tuple-element.52) | copy-start | bytes 73732
  272.7 7.9 %copy-start.5 = (f32[1,6144]{1,0:T(1,128)S(1)}, f32[1,6144]{1,0:T(1,128)}, u32[]{:S(2)}) copy-start(f32[1,6144]{1,0:T(1,128)} %get-tuple-element.53) | copy-start | bytes 73732
  272.7 7.9 %copy-start.6 = (f32[1,6144]{1,0:T(1,128)S(1)}, f32[1,6144]{1,0:T(1,128)}, u32[]{:S(2)}) copy-start(f32[1,6144]{1,0:T(1,128)} %get-tuple-element.54) | copy-start | bytes 73732
  272.7 7.9 %copy-start.7 = (f32[1,6144]{1,0:T(1,128)S(1)}, f32[1,6144]{1,0:T(1,128)}, u32[]{:S(2)}) copy-start(f32[1,6144]{1,0:T(1,128)} %get-tuple-element.55) | copy-start | bytes 73732
  272.8 7.9 %copy-start.8 = (f32[1,6144]{1,0:T(1,128)S(1)}, f32[1,6144]{1,0:T(1,128)}, u32[]{:S(2)}) copy-start(f32[1,6144]{1,0:T(1,128)} %get-tuple-element.56) | copy-start | bytes 73732
  272.8 7.9 %copy-start.9 = (f32[1,6144]{1,0:T(1,128)S(1)}, f32[1,6144]{1,0:T(1,128)}, u32[]{:S(2)}) copy-start(f32[1,6144]{1,0:T(1,128)} %get-tuple-element.57) | copy-start | bytes 73732
  272.8 7.9 %copy-start.10 = (f32[1,6144]{1,0:T(1,128)S(1)}, f32[1,6144]{1,0:T(1,128)}, u32[]{:S(2)}) copy-start(f32[1,6144]{1,0:T(1,128)} %get-tuple-element.58) | copy-start | bytes 73732
  272.8 7.9 %copy-start.11 = (f32[1,6144]{1,0:T(1,128)S(1)}, f32[1,6144]{1,0:T(1,128)}, u32[]{:S(2)}) copy-start(f32[1,6144]{1,0:T(1,128)} %get-tuple-element.59) | copy-start | bytes 73732
  272.8 7.9 %copy-start.12 = (f32[1,6144]{1,0:T(1,128)S(1)}, f32[1,6144]{1,0:T(1,128)}, u32[]{:S(2)}) copy-start(f32[1,6144]{1,0:T(1,128)} %get-tuple-element.60) | copy-start | bytes 73732
  272.8 7.9 %copy-start.13 = (f32[1,6144]{1,0:T(1,128)S(1)}, f32[1,6144]{1,0:T(1,128)}, u32[]{:S(2)}) copy-start(f32[1,6144]{1,0:T(1,128)} %get-tuple-element.61) | copy-start | bytes 73732
  272.8 7.9 %copy-start.14 = (f32[1,6144]{1,0:T(1,128)S(1)}, f32[1,6144]{1,0:T(1,128)}, u32[]{:S(2)}) copy-start(f32[1,6144]{1,0:T(1,128)} %get-tuple-element.62) | copy-start | bytes 73732
  272.8 7.9 %copy-start.15 = (f32[1,6144]{1,0:T(1,128)S(1)}, f32[1,6144]{1,0:T(1,128)}, u32[]{:S(2)}) copy-start(f32[1,6144]{1,0:T(1,128)} %get-tuple-element.63) | copy-start | bytes 73732
  272.8 7.9 %copy-start.16 = (f32[1,6144]{1,0:T(1,128)S(1)}, f32[1,6144]{1,0:T(1,128)}, u32[]{:S(2)}) copy-start(f32[1,6144]{1,0:T(1,128)} %get-tuple-element.64) | copy-start | bytes 73732
  272.8 7.9 %copy-start.17 = (f32[1,6144]{1,0:T(1,128)S(1)}, f32[1,6144]{1,0:T(1,128)}, u32[]{:S(2)}) copy-start(f32[1,6144]{1,0:T(1,128)} %get-tuple-element.65) | copy-start | bytes 73732
Sparse Core Ops, SparseCore 0:
  280.8 269.7 reduce-scatter.3
where the time goes:
time: 572 us; the launch traced here: 571 us
  blocking collectives  183 us (32%)
  waiting for transfers between devices  182 us (32%)
  other arithmetic  179 us (31%)
  between operations  14.3 us (2%)
  local copies, waits for them, and re-layouts  13.4 us (2%)
    unnamed x2, waiting for transfers between devices  182 us
    all_gather x1, blocking collectives, per_device(): gathered = lax.all_gather(packed, 'shard', axis=1, tiled=True)  171 us
    convert_element_type x1, other arithmetic, backward_part(): return (grad_input.astype(jnp.bfloat16), terms)  88 us
    reduce_sum x1, other arithmetic, forward_part(): row_mean = jnp.mean(conv_out, axis=-1, keepdims=True)  37.1 us
    reduce_sum x4, other arithmetic, backward_part(): jnp.sum(grad_conv * padded_in[lag_index:lag_index + length].astype(jnp.fl...  33.4 us
    psum x1, blocking collectives, per_device(): summed = lax.psum(share_sum, 'rep')  11.9 us
  transfers between devices with their start and end apart: 1, of which 1 were waited for; matrix products, arithmetic and copies ran while one was open for 15% of the time, Pallas kernels for 0%

commit v1 on v0

--- a/solution.py
+++ b/solution.py
@@ -66,7 +66,10 @@
 def per_device(conv_input, cotangent, kernel, conv_bias, ln_gain, ln_bias):
     taps = kernel.shape[0]
     packed = jnp.concatenate([kernel, conv_bias[None], ln_gain[None], ln_bias[None]], 0)
-    gathered = lax.all_gather(packed, "shard", axis=1, tiled=True)
+    peers = lax.axis_size("shard")
+    blocks = jnp.stack([packed for _ in range(peers)])
+    blocks = lax.all_to_all(blocks, "shard", split_axis=0, concat_axis=0)
+    gathered = jnp.concatenate(blocks, axis=1)
     activated, normed, inverse, affine, squash = jax.vmap(forward_part, in_axes=(0, None))(
         conv_input, gathered
     )

time: 572 us -> 637 us (1.11)
  local copies, waits for them, and re-layouts: 13.4 us -> 48.7 us
  starting transfers between devices: 0.04 us -> 15.4 us
  other arithmetic: 179 us -> 186 us
    convert_element_type x0 -> x34, local copies, waits for them, and re-layouts: none -> 34.6 us  [the longest x30 29.4 us: forward_part(): params[lag_index].astype(jnp.float32)]
    all_to_all x0 -> x1, starting transfers between devices: none -> 15.3 us  [per_device(): blocks = lax.all_to_all(blocks, 'shard', split_axis=0, concat_axis=0)]
  transfers between devices with their start and end apart: 1 -> 2, of which waited for: 1 -> 1; matrix products, arithmetic and copies ran while one was open for 15% -> 15% of each run, Pallas kernels for 0% -> 0%
where the time goes in v1:
time: 637 us; the launch traced here: 634 us
  other arithmetic  186 us (29%)
  blocking collectives  185 us (29%)
  waiting for transfers between devices  185 us (29%)
  local copies, waits for them, and re-layouts  48.7 us (8%)
  starting transfers between devices  15.4 us (2%)
  between operations  14.7 us (2%)
    unnamed x2, waiting for transfers between devices  185 us
    all_gather x1, blocking collectives, per_device(): again = lax.all_gather(packed, 'shard', axis=1, tiled=True)  173 us
    convert_element_type x1, other arithmetic, backward_part(): return (grad_input.astype(jnp.bfloat16), terms)  88.1 us
    reduce_sum x1, other arithmetic, forward_part(): row_mean = jnp.mean(conv_out, axis=-1, keepdims=True)  37.7 us
    reduce_sum x4, other arithmetic, backward_part(): jnp.sum(grad_conv * padded_in[lag_index:lag_index + length].astype(jnp.fl...  32.1 us
    convert_element_type x30, local copies, waits for them, and re-layouts, forward_part(): params[lag_index].astype(jnp.float32)  29.4 us
    all_to_all x1, starting transfers between devices, per_device(): blocks = lax.all_to_all(blocks, 'shard', split_axis=0, concat_axis=0)  15.3 us
  transfers between devices with their start and end apart: 2, of which 1 were waited for; matrix products, arithmetic and copies ran while one was open for 15% of the time, Pallas kernels for 0%

profile of v1, /device:TPU:1, one launch (start us, length us, event | category | flops | bytes accessed | tf_op | source)
XLA Modules:
  0.0 634.2 jit_solution(2301838018589365052)
XLA Ops:
  7.2 0.9 fusion.157
  8.1 0.9 stack.66
  9.0 15.3 %all-to-all-start = ((bf16[64,34,96]{2,1,0:T(8,128)(2,1)}), bf16[64,34,96]{2,1,0:T(8,128)(2,1)}, u32[]{:S(2)}, u32[]{:S(2)}) async-start(bf16[64,34,96]{2,1,0:T(8,128)(2,1)} %stack.66), calls=%async_computation | async-start | bytes 1310720 | tf_op jit(solution)/shard_map/all_to_all | solution.py:71
  24.4 0.0 reduce-scatter.4.cloned.1.call-start
  24.4 172.7 %all-gather = bf16[64,96,34]{1,2,0:T(8,128)(2,1)S(1)} all-gather(bf16[1,96,34]{1,2,0:T(8,128)(2,1)S(1)} %get-tuple-element.116), channel_id=1, replica_groups=mesh['rep'=4,'shard'=64] {'shard'}, dimensions={0}, use_global_device_ids=true | all-gather | bytes 424320 | tf_op jit(solution)/shard_map/all_gather | solution.py:76
  197.1 0.9 copy.13
  198.0 2.7 reshape.857
  200.7 3.0 slice_convert_fusion.65
  203.7 2.6 slice_convert_fusion.63
  206.3 0.0 all-to-all-done
  206.3 4.5 fusion.155
  210.8 4.7 fusion.156
  215.5 0.8 reshape.790
  216.4 1.4 reshape.791
  217.8 1.4 reshape.806
  219.2 1.4 reshape.805
  220.7 1.4 reshape.804
  222.1 1.4 reshape.803
  223.6 1.4 reshape.802
  225.0 1.4 reshape.801
  226.4 1.4 reshape.800
  227.9 1.4 reshape.799
  229.3 1.4 reshape.798
  230.7 1.4 reshape.797
  232.2 1.4 reshape.796
  233.6 1.4 reshape.795
  235.1 1.4 reshape.794
  236.5 1.4 reshape.793
  237.9 1.4 reshape.792
  239.4 1.4 reshape.823
  240.8 1.4 reshape.822
  242.3 1.4 reshape.821
  243.7 1.4 reshape.820
  245.1 1.4 reshape.819
  246.6 1.4 reshape.818
  248.0 0.7 reshape.817
  248.7 0.1 reshape.816
  248.8 0.1 reshape.815
  248.9 0.1 reshape.814
  249.0 0.1 reshape.813
  249.0 0.1 reshape.812
  249.1 0.1 reshape.811
  249.2 0.1 reshape.810
  249.3 0.1 reshape.809
  249.4 0.1 reshape.808
  249.5 0.7 reshape.807
  250.1 37.7 %fusion.158 = (f32[256]{0:T(256)S(1)}, f32[1,256,6144]{2,1,0:T(8,128)}) fusion(f32[6144]{0:T(1024)} %reshape.822, f32[6144]{0:T(1024)} %reshape.821, f32[6144]{0:T(1024)} %reshape.820, f32[6144]{0:T(1024)} %reshape.819, f32[6144]{0:T(1024)} %reshape.818, f32[6144]{0:T(1024)} %reshape.817, f32[6144]{0:T(1024)S(1)} %reshape.816, f32[6144]{0:T(1024)S(1)} %reshape.815, ...), kind=kLoop, calls=%fused_computation.336 | loop fusion | flops 147848960 | bytes 10224640 | tf_op jit(solution)/shard_map/vmap()/reduce_sum | solution.py:20
  287.9 3.7 multiply_reduce_fusion.2
  291.6 0.9 copy-done.1
  292.5 8.6 %multiply_reduce_fusion = (f32[6144]{0:T(1024)S(1)}, f32[256]{0:T(256)S(1)}, f32[256]{0:T(256)S(1)}, f32[6144]{0:T(1024)S(1)}, f32[1,256,6144]{2,1,0:T(8,128)S(1)}, /*index=5*/bf16[1,256,6144]{2,1,0:T(8,128)(2,1)}) fusion(f32[1,256,6144]{2,1,0:T(8,128)S(1)} %copy-done.1, f32[256]{0:T(256)S(1)} %add_rsqrt_fusion, f32[256]{0:T(256)S(1)} %broadcast_multiply_fusion.3, ...), kind=kLoop, calls=%fused_computation.215 | loop fusion | flops 34590208 | bytes 19001344 | tf_op jit(solution)/shard_map/vmap()/reduce_sum | solution.py:58
  301.1 11.6 %fusion.122 = (f32[6144]{0:T(1024)}, f32[6144]{0:T(1024)}, f32[6144]{0:T(1024)}, f32[6144]{0:T(1024)}, f32[6144]{0:T(1024)}, /*index=5*/f32[6144]{0:T(1024)}, f3...) fusion(bf16[1,256,6144]{2,1,0:T(8,128)(2,1)S(1)} %copy-done.2, f32[256]{0:T(256)S(1)} %get-tuple-element.118, ...), kind=kLoop, calls=%fused_computation.214 | loop fusion | flops 53422080 | bytes 22269952 | tf_op jit(solution)/shard_map/vmap()/reduce_sum | solution.py:43
  312.7 3.6 fusion.89
  316.4 8.5 %fusion.98 = (f32[6144]{0:T(1024)}, f32[6144]{0:T(1024)}, f32[6144]{0:T(1024)}, f32[6144]{0:T(1024)}, f32[6144]{0:T(1024)}, /*index=5*/f32[6144]{0:T(1024)}, f32[6144]{0:T(1024)}, f32[6144]{0:T(1024)}, f32[6144]{0:T(1024)}) fusion(f32[1,256,6144]{2,1,0:T(8,128)S(1)} %get-tuple-element.76, bf16[1,256,6144]{2,1,0:T(8,128)(2,1)S(1)} %copy-done.2), kind=kLoop, calls=%fused_computation.190 | loop fusion | flops 42412032 | bytes 9658368 | tf_op jit(solution)/shard_map/vmap()/reduce_sum | solution.py:43
  324.9 8.3 %fusion.107 = (f32[6144]{0:T(1024)S(1)}, f32[6144]{0:T(1024)S(1)}, f32[6144]{0:T(1024)S(1)}, f32[6144]{0:T(1024)S(1)}, f32[6144]{0:T(1024)S(1)}, /*index=5*/f32[...) fusion(f32[1,256,6144]{2,1,0:T(8,128)S(1)} %get-tuple-element.76, ...), kind=kLoop, calls=%fused_computation.199 | loop fusion | flops 43978752 | bytes 9682944 | tf_op jit(solution)/shard_map/vmap()/reduce_sum | solution.py:43
  333.5 4.3 stack.195
  337.9 0.1 maximum_bitcast_fusion
  338.0 2.3 copy.14
  340.3 0.0 reduce-scatter.4.cloned.1.call-update
  340.6 88.1 %fusion.54 = bf16[1,256,6144]{2,1,0:T(8,128)(2,1)} fusion(f32[1,256,6144]{2,1,0:T(8,128)} %copy-done, f32[6144]{0:T(1024)S(1)} %bitcast.123, f32[6144]{0:T(1024)S(1)} %bitcast.124, f32[6144]{0:T(1024)S(1)} %bitcast.125, f32[6144]{0:T(1024)S(1)} %bitcast.126, f32[6144]{0:T(1024)S(1)} %bitcast.127, f32[6144]{0:T(1024)S(1)} %bitcast.128, ...), kind=kLoop, calls=%fused_computation.146 | loop fusion | flops 97517568 | bytes 10199040 | tf_op jit(solution)/shard_map/vmap()/convert_element_type | solution.py:63
  428.7 184.8 %reduce-scatter.4.cloned.1.call-done = f32[96,34]{1,0:T(8,128)} async-done(((f32[6144,34]{1,0:T(8,128)}), f32[96,34]{1,0:T(8,128)}) %reduce-scatter.4.cloned.1.call-update) | async-done | bytes 13072
  613.5 0.9 copy.15
  614.3 11.9 %psum.7 = f32[34,96]{1,0:T(8,128)S(1)} all-reduce(f32[34,96]{1,0:T(8,128)S(1)} %copy.15), channel_id=1, replica_groups=mesh['rep'=4,'shard'=64] {'rep'}, use_global_device_ids=true, to_apply=%region_39.40 | all-reduce | flops 3264 | bytes 26112 | tf_op jit(solution)/shard_map/psum | solution.py:84
  626.2 0.5 slice_bitcast_fusion
  626.7 0.6 slice.653
  (73 shorter events, 0.2 us)
Async XLA Ops:
  7.2 243.0 %copy-start.2 = (bf16[1,256,6144]{2,1,0:T(8,128)(2,1)S(1)}, bf16[1,256,6144]{2,1,0:T(8,128)(2,1)}, u32[]{:S(2)}) copy-start(bf16[1,256,6144]{2,1,0:T(8,128)(2,1)} %param.6) | copy-start | bytes 9437188
  9.0 197.3 %all-to-all-start = ((bf16[64,34,96]{2,1,0:T(8,128)(2,1)}), bf16[64,34,96]{2,1,0:T(8,128)(2,1)}, u32[]{:S(2)}, u32[]{:S(2)}) async-start(bf16[64,34,96]{2,1,0:T(8,128)(2,1)} %stack.66), calls=%async_computation | async-start | bytes 1310720 | tf_op jit(solution)/shard_map/all_to_all | solution.py:71
  24.4 589.1 %reduce-scatter.4.cloned.1.call-start = ((), (), s32[]{:S(2)}) async-start(), calls=%async_computation.2 | async-start | bytes 3194880
  250.1 41.5 %copy-start.3 = (f32[6144]{0:T(1024)S(1)}, f32[6144]{0:T(1024)}, u32[]{:S(2)}) copy-start(f32[6144]{0:T(1024)} %reshape.823) | copy-start | bytes 73732
  287.9 4.6 copy-start.1
  312.7 12.2 %copy-start = (f32[1,256,6144]{2,1,0:T(8,128)}, f32[1,256,6144]{2,1,0:T(8,128)S(1)}, u32[]{:S(2)}) copy-start(f32[1,256,6144]{2,1,0:T(8,128)S(1)} %get-tuple-element.76) | copy-start | bytes 18874372
  333.2 7.1 %copy-start.4 = (f32[1,6144]{1,0:T(1,128)S(1)}, f32[1,6144]{1,0:T(1,128)}, u32[]{:S(2)}) copy-start(f32[1,6144]{1,0:T(1,128)} %get-tuple-element.100) | copy-start | bytes 73732
  333.2 7.1 %copy-start.5 = (f32[1,6144]{1,0:T(1,128)S(1)}, f32[1,6144]{1,0:T(1,128)}, u32[]{:S(2)}) copy-start(f32[1,6144]{1,0:T(1,128)} %get-tuple-element.101) | copy-start | bytes 73732
  333.2 7.1 %copy-start.6 = (f32[1,6144]{1,0:T(1,128)S(1)}, f32[1,6144]{1,0:T(1,128)}, u32[]{:S(2)}) copy-start(f32[1,6144]{1,0:T(1,128)} %get-tuple-element.102) | copy-start | bytes 73732
  333.3 7.1 %copy-start.7 = (f32[1,6144]{1,0:T(1,128)S(1)}, f32[1,6144]{1,0:T(1,128)}, u32[]{:S(2)}) copy-start(f32[1,6144]{1,0:T(1,128)} %get-tuple-element.103) | copy-start | bytes 73732
  333.3 7.1 %copy-start.8 = (f32[1,6144]{1,0:T(1,128)S(1)}, f32[1,6144]{1,0:T(1,128)}, u32[]{:S(2)}) copy-start(f32[1,6144]{1,0:T(1,128)} %get-tuple-element.104) | copy-start | bytes 73732
  333.3 7.1 %copy-start.9 = (f32[1,6144]{1,0:T(1,128)S(1)}, f32[1,6144]{1,0:T(1,128)}, u32[]{:S(2)}) copy-start(f32[1,6144]{1,0:T(1,128)} %get-tuple-element.105) | copy-start | bytes 73732
  333.3 7.1 %copy-start.10 = (f32[1,6144]{1,0:T(1,128)S(1)}, f32[1,6144]{1,0:T(1,128)}, u32[]{:S(2)}) copy-start(f32[1,6144]{1,0:T(1,128)} %get-tuple-element.106) | copy-start | bytes 73732
  333.3 7.1 %copy-start.11 = (f32[1,6144]{1,0:T(1,128)S(1)}, f32[1,6144]{1,0:T(1,128)}, u32[]{:S(2)}) copy-start(f32[1,6144]{1,0:T(1,128)} %get-tuple-element.107) | copy-start | bytes 73732
  333.3 7.1 %copy-start.12 = (f32[1,6144]{1,0:T(1,128)S(1)}, f32[1,6144]{1,0:T(1,128)}, u32[]{:S(2)}) copy-start(f32[1,6144]{1,0:T(1,128)} %get-tuple-element.108) | copy-start | bytes 73732
  333.3 7.1 %copy-start.13 = (f32[1,6144]{1,0:T(1,128)S(1)}, f32[1,6144]{1,0:T(1,128)}, u32[]{:S(2)}) copy-start(f32[1,6144]{1,0:T(1,128)} %get-tuple-element.109) | copy-start | bytes 73732
  333.3 7.1 %copy-start.14 = (f32[1,6144]{1,0:T(1,128)S(1)}, f32[1,6144]{1,0:T(1,128)}, u32[]{:S(2)}) copy-start(f32[1,6144]{1,0:T(1,128)} %get-tuple-element.110) | copy-start | bytes 73732
  333.3 7.1 %copy-start.15 = (f32[1,6144]{1,0:T(1,128)S(1)}, f32[1,6144]{1,0:T(1,128)}, u32[]{:S(2)}) copy-start(f32[1,6144]{1,0:T(1,128)} %get-tuple-element.111) | copy-start | bytes 73732
  333.3 7.1 %copy-start.16 = (f32[1,6144]{1,0:T(1,128)S(1)}, f32[1,6144]{1,0:T(1,128)}, u32[]{:S(2)}) copy-start(f32[1,6144]{1,0:T(1,128)} %get-tuple-element.81) | copy-start | bytes 73732
  333.4 7.1 %copy-start.17 = (f32[1,6144]{1,0:T(1,128)S(1)}, f32[1,6144]{1,0:T(1,128)}, u32[]{:S(2)}) copy-start(f32[1,6144]{1,0:T(1,128)} %get-tuple-element.82) | copy-start | bytes 73732
  333.4 7.1 %copy-start.18 = (f32[1,6144]{1,0:T(1,128)S(1)}, f32[1,6144]{1,0:T(1,128)}, u32[]{:S(2)}) copy-start(f32[1,6144]{1,0:T(1,128)} %get-tuple-element.83) | copy-start | bytes 73732
  333.4 7.1 %copy-start.19 = (f32[1,6144]{1,0:T(1,128)S(1)}, f32[1,6144]{1,0:T(1,128)}, u32[]{:S(2)}) copy-start(f32[1,6144]{1,0:T(1,128)} %get-tuple-element.84) | copy-start | bytes 73732
  333.4 7.1 %copy-start.20 = (f32[1,6144]{1,0:T(1,128)S(1)}, f32[1,6144]{1,0:T(1,128)}, u32[]{:S(2)}) copy-start(f32[1,6144]{1,0:T(1,128)} %get-tuple-element.85) | copy-start | bytes 73732
  333.4 7.1 %copy-start.21 = (f32[1,6144]{1,0:T(1,128)S(1)}, f32[1,6144]{1,0:T(1,128)}, u32[]{:S(2)}) copy-start(f32[1,6144]{1,0:T(1,128)} %get-tuple-element.86) | copy-start | bytes 73732
  333.4 7.1 %copy-start.22 = (f32[1,6144]{1,0:T(1,128)S(1)}, f32[1,6144]{1,0:T(1,128)}, u32[]{:S(2)}) copy-start(f32[1,6144]{1,0:T(1,128)} %get-tuple-element.87) | copy-start | bytes 73732
  333.4 7.1 %copy-start.23 = (f32[1,6144]{1,0:T(1,128)S(1)}, f32[1,6144]{1,0:T(1,128)}, u32[]{:S(2)}) copy-start(f32[1,6144]{1,0:T(1,128)} %get-tuple-element.88) | copy-start | bytes 73732
  333.4 7.1 %copy-start.24 = (f32[1,6144]{1,0:T(1,128)S(1)}, f32[1,6144]{1,0:T(1,128)}, u32[]{:S(2)}) copy-start(f32[1,6144]{1,0:T(1,128)} %get-tuple-element.89) | copy-start | bytes 73732
  333.4 7.1 %copy-start.25 = (f32[1,6144]{1,0:T(1,128)S(1)}, f32[1,6144]{1,0:T(1,128)}, u32[]{:S(2)}) copy-start(f32[1,6144]{1,0:T(1,128)} %get-tuple-element.90) | copy-start | bytes 73732
  333.4 7.1 %copy-start.26 = (f32[1,6144]{1,0:T(1,128)S(1)}, f32[1,6144]{1,0:T(1,128)}, u32[]{:S(2)}) copy-start(f32[1,6144]{1,0:T(1,128)} %get-tuple-element.91) | copy-start | bytes 73732
  333.5 7.1 %copy-start.27 = (f32[1,6144]{1,0:T(1,128)S(1)}, f32[1,6144]{1,0:T(1,128)}, u32[]{:S(2)}) copy-start(f32[1,6144]{1,0:T(1,128)} %get-tuple-element.92) | copy-start | bytes 73732
  333.5 7.1 %copy-start.28 = (f32[1,6144]{1,0:T(1,128)S(1)}, f32[1,6144]{1,0:T(1,128)}, u32[]{:S(2)}) copy-start(f32[1,6144]{1,0:T(1,128)} %get-tuple-element.93) | copy-start | bytes 73732
  333.5 7.1 %copy-start.29 = (f32[1,6144]{1,0:T(1,128)S(1)}, f32[1,6144]{1,0:T(1,128)}, u32[]{:S(2)}) copy-start(f32[1,6144]{1,0:T(1,128)} %get-tuple-element.94) | copy-start | bytes 73732
  333.5 7.1 %copy-start.30 = (f32[1,6144]{1,0:T(1,128)S(1)}, f32[1,6144]{1,0:T(1,128)}, u32[]{:S(2)}) copy-start(f32[1,6144]{1,0:T(1,128)} %get-tuple-element.95) | copy-start | bytes 73732
  333.5 7.1 %copy-start.31 = (f32[1,6144]{1,0:T(1,128)S(1)}, f32[1,6144]{1,0:T(1,128)}, u32[]{:S(2)}) copy-start(f32[1,6144]{1,0:T(1,128)} %get-tuple-element.96) | copy-start | bytes 73732
  333.5 7.1 %copy-start.32 = (f32[1,6144]{1,0:T(1,128)S(1)}, f32[1,6144]{1,0:T(1,128)}, u32[]{:S(2)}) copy-start(f32[1,6144]{1,0:T(1,128)} %get-tuple-element.97) | copy-start | bytes 73732
  333.5 7.1 %copy-start.33 = (f32[1,6144]{1,0:T(1,128)S(1)}, f32[1,6144]{1,0:T(1,128)}, u32[]{:S(2)}) copy-start(f32[1,6144]{1,0:T(1,128)} %get-tuple-element.98) | copy-start | bytes 73732
  333.5 7.1 %copy-start.34 = (f32[1,6144]{1,0:T(1,128)S(1)}, f32[1,6144]{1,0:T(1,128)}, u32[]{:S(2)}) copy-start(f32[1,6144]{1,0:T(1,128)} %get-tuple-element.99) | copy-start | bytes 73732
Sparse Core Ops, SparseCore 0:
  340.5 272.9 reduce-scatter.3
